TPU v7x, 32 devices: a whole 2x2x4 slice. The times are simulated.
32 devices in a mesh: stream: 16 (over z, y, core), span: 2 (over x).
Axes of the slice: x: 2, y: 2, z: 4, core: 2. Of those that a mesh axis runs over, the one named last changes fastest.
Arguments:
- rhs: float32 [64, 2, 320], P('stream', 'span'), may hold values from -1.5 to 1.5
- lower_block: float32 [64, 2, 320, 320], P('stream', 'span'), may hold values from -1.2 to 0.2
- upper_block: bfloat16 [64, 2, 320, 320], P('stream', 'span'), may hold values from -0.099609375 to 0.099609375
- span_block: bfloat16 [64, 2, 2, 320, 320], P('stream', 'span'), may hold values from -0.099609375 to 0.099609375
Outputs:
- preconditioned: float32 [64, 2, 320], P('stream', 'span')
All inputs are finite; a program needn't handle non-finite values.
Results may differ from a plain program's by a relative error of at most 0.0003.
Values sent between devices are 32-bit elements; how exact they have to be, the bound alone decides.
A program may use at most 128 MiB of HBM per device.

v0:
```python
import jax
import jax.numpy as jnp
from jax import lax
from jax.sharding import PartitionSpec as P


def carried_in(x, axis, combine, identity):
    length, place = (lax.axis_size(axis), lax.axis_index(axis))
    everything = jax.tree.map(lambda part: lax.all_gather(part, axis), x)
    start = jax.tree.map(
        lambda part, zero: jnp.broadcast_to(jnp.asarray(zero, part.dtype), part.shape), x, identity
    )

    def hop(k, before):
        reached = k < place
        new = combine(before, jax.tree.map(lambda part: part[k], everything))
        return jax.tree.map(lambda a, b: jnp.where(reached, a, b), new, before)

    return lax.fori_loop(0, length, hop, start)


def spread(value, axis, source):
    kept = jnp.where(lax.axis_index(axis) == source, value, 0).astype(value.dtype)
    return lax.psum(kept, axis)


def passed_along(x, axis, by):
    length = lax.axis_size(axis)
    return lax.ppermute(x, axis, [(i, (i + by) % length) for i in range(length)])


def padded_2(block, sides, width):
    for axis, dim in sides:
        count = lax.axis_size(axis)
        forward = [(i, i + 1) for i in range(count - 1)]
        forward.append((count - 1, 0))
        backward = [(target, source) for source, target in forward]
        low = lax.ppermute(
            lax.slice_in_dim(block, block.shape[dim] - width, None, axis=dim), axis, forward
        )
        high = lax.ppermute(lax.slice_in_dim(block, 0, width, axis=dim), axis, backward)
        block = jnp.concatenate([low, block, high], axis=dim)
    return block


def apply_block(blocks, vector):
    return jnp.einsum(
        "...bc,...c->...b", blocks.astype(jnp.float32), vector, precision=lax.Precision.HIGHEST
    )


def compose(later, earlier):
    return jnp.einsum("lbc,lcd->lbd", later, earlier, precision=lax.Precision.HIGHEST)


def slab_chain(offsets, lower_blocks, start):
    results = []
    state = start
    for slab in range(offsets.shape[0]):
        state = offsets[slab] - apply_block(lower_blocks[slab], state)
        results.append(state)
    return jnp.stack(results)


def local_mapping(lower_blocks):
    mapping = -lower_blocks[0]
    for slab in range(1, lower_blocks.shape[0]):
        mapping = -compose(lower_blocks[slab], mapping)
    return mapping


def combine(earlier, later):
    map_early, shift_early = earlier
    late_mapping, shift_late = later
    return (compose(late_mapping, map_early), apply_block(late_mapping, shift_early) + shift_late)


def incoming(offsets, lower_blocks, wrap_state, has_wrap):
    zero_state = jnp.zeros(offsets.shape[1:], jnp.float32)
    mapping = local_mapping(lower_blocks)
    shift_part = slab_chain(offsets, lower_blocks, zero_state)[-1]
    identity = (
        jnp.broadcast_to(jnp.eye(mapping.shape[1], dtype=jnp.float32), mapping.shape),
        zero_state,
    )
    prefix_map, partial_sum_offset = carried_in((mapping, shift_part), "stream", combine, identity)
    if has_wrap:
        return apply_block(prefix_map, wrap_state) + partial_sum_offset
    return partial_sum_offset


def shards(rhs, lower_block, upper_block, span_block):
    zero_state = jnp.zeros(rhs.shape[1:], jnp.float32)
    start_one = incoming(rhs, lower_block, zero_state, False)
    first = slab_chain(rhs, lower_block, start_one)
    wrap_state = spread(first[-1], "stream", lax.axis_size("stream") - 1)
    following_initial = passed_along(first[0], "stream", -1)
    downstream = jnp.concatenate([first[1:], following_initial[None]], axis=0)
    padded = padded_2(first, (("span", 1),), 1)
    below = padded[:, :-2]
    above = padded[:, 2:]
    offsets = rhs - apply_block(upper_block, downstream)
    offsets = (
        offsets - apply_block(span_block[:, :, 0], below) - apply_block(span_block[:, :, 1], above)
    )
    start_two = incoming(offsets, lower_block, wrap_state, True)
    return slab_chain(offsets, lower_block, start_two)


def solution(mesh):
    return jax.shard_map(
        shards,
        mesh=mesh,
        in_specs=(
            P("stream", "span", None),
            P("stream", "span", None, None),
            P("stream", "span", None, None),
            P("stream", "span", None, None, None),
        ),
        out_specs=P("stream", "span", None),
        check_vma=False,
    )
```

profile of v0, /device:TPU:0, one launch (start us, length us, event | category | flops | bytes accessed | tf_op | source)
XLA Modules:
  0.0 260.8 jit_solution(4759402616321688188)
XLA Ops:
  6.5 2.4 convolution_negate_fusion.2
  9.0 3.0 %convolution_negate_fusion.1 = f32[320,320]{1,0:T(8,128)S(1)} fusion(f32[320,320]{1,0:T(8,128)S(1)} %convolution_negate_fusion.2, f32[4,1,320,320]{3,2,1,0:T(8,128)} %param.9), kind=kOutput, calls=%fused_computation.26 | convolution fusion | flops 393318400 | bytes 1310720 | tf_op jit(solution)/shard_map/lbc,lcd->lbd/dot_general | solution.py:53
  12.0 1.9 fusion.15
  13.9 2.0 copy.7
  19.5 64.5 %all-reduce = f32[5120]{0:T(1024)S(1)} all-reduce(f32[5120]{0:T(1024)S(1)} %subtract_dynamic-update-slice_fusion.1), channel_id=3, replica_groups=mesh['stream'=16,'span'=2] {'stream'}, use_global_device_ids=true, to_apply=%add | all-reduce | flops 5120 | bytes 40960
  84.2 6.8 %all-gather.5.cloned.1.call-done = f32[5120,320]{1,0:T(8,128)} async-done(((f32[320,320]{1,0:T(8,128)}), f32[5120,320]{1,0:T(8,128)}) %all-gather.5.cloned.1.call-update) | async-done | bytes 6553616 | tf_op jit(solution)/shard_map/all_gather | solution.py:9
  91.0 26.4 %while.30 = (s32[]{:T(128)}, f32[1,320]{1,0:T(1,128)S(1)}, s32[]{:T(128)}, f32[16,1,320,320]{3,2,1,0:T(8,128)}, f32[16,1,320]{2,1,0:T(1,128)S(1)}, /*index=5*/s32[]{:T(128)}, s32[]{:T(128)}) while((s32[]{:T(128)}, f32[1,320]{1,0:T(1,128)S(1)}, s32[]{:T(128)}, f32[16,1,320,320]{3,2,1,0:T(8,128)}, f32[16,1,320]{2,1,0:T(1,128)S(1)}, ...), condition=%wide.region_1.2_spmd.clone, body=%wide.region_0.1_spmd.clone.sunk | while | flops 1230084 | bytes 504434 | solution.py:19
  92.6 1.6 convolution_reduce_fusion.19
  94.3 1.6 convolution_reduce_fusion.19
  95.9 1.6 convolution_reduce_fusion.19
  97.6 1.6 convolution_reduce_fusion.19
  99.2 1.6 convolution_reduce_fusion.19
  100.9 1.6 convolution_reduce_fusion.19
  102.5 1.6 convolution_reduce_fusion.19
  104.2 1.6 convolution_reduce_fusion.19
  105.8 1.6 convolution_reduce_fusion.19
  107.5 1.6 convolution_reduce_fusion.19
  109.1 1.6 convolution_reduce_fusion.19
  110.8 1.6 convolution_reduce_fusion.19
  112.4 1.6 convolution_reduce_fusion.19
  114.1 1.6 convolution_reduce_fusion.19
  115.7 1.6 convolution_reduce_fusion.19
  119.6 1.7 collective-permute-start
  129.3 60.0 %all-reduce.2 = (f32[5120]{0:T(1024)S(1)}, f32[320]{0:T(512)S(1)}) all-reduce(f32[5120]{0:T(1024)S(1)} %subtract_dynamic-update-slice_fusion, f32[320]{0:T(512)S(1)} %get-tuple-element.305), channel_id=4, replica_groups=mesh['stream'=16,'span'=2] {'stream'}, use_global_device_ids=true, to_apply=%add.1 | all-reduce | flops 5440 | bytes 43520
  189.4 61.2 %while.31 = (s32[]{:T(128)}, f32[1,320,320]{2,1,0:T(8,128)S(1)}, f32[1,320]{1,0:T(1,128)S(1)}, s32[]{:T(128)}, f32[16,1,320,320]{3,2,1,0:T(8,128)}, /*index=5*/f32[16,1,320]{2,1,0:T(1,128)S(1)}, s32[]{:T(128)}, s32[]{:T(128)}) while((s32[]{:T(128)}, f32[1,320,320]{2,1,0:T(8,128)S(1)}, f32[1,320]{1,0:T(1,128)S(1)}, s32[]{:T(128)}, ...), condition=%wide.region_3.4_spmd.clone, body=%wide.region_2.3_spmd.clone.sunk | while | flops 394548480 | bytes 3207807 | solution.py:19
  189.4 1.6 convolution_reduce_fusion.20
  191.0 2.1 fusion.107
  194.9 2.1 fusion.107
  198.7 2.1 fusion.107
  200.9 1.6 convolution_reduce_fusion.20
  202.5 2.1 fusion.107
  206.3 2.1 fusion.107
  210.2 2.1 fusion.107
  212.4 1.6 convolution_reduce_fusion.20
  214.0 2.1 fusion.107
  217.8 2.1 fusion.107
  220.0 1.6 convolution_reduce_fusion.20
  221.6 2.1 fusion.107
  225.4 2.1 fusion.107
  227.7 1.6 convolution_reduce_fusion.20
  229.3 2.1 fusion.107
  233.1 2.1 fusion.107
  235.3 1.6 convolution_reduce_fusion.20
  236.9 2.1 fusion.107
  240.7 2.1 fusion.107
  243.0 1.6 convolution_reduce_fusion.20
  244.6 2.1 fusion.107
  248.4 2.1 fusion.107
  (214 shorter events, 34.1 us)
Async XLA Ops:
  6.5 117.0 %copy-start = (bf16[4,1,320,320]{3,2,1,0:T(8,128)(2,1)S(1)}, bf16[4,1,320,320]{3,2,1,0:T(8,128)(2,1)}, u32[]{:S(2)}) copy-start(bf16[4,1,320,320]{3,2,1,0:T(8,128)(2,1)} %param.10) | copy-start | bytes 2457604
  6.5 5.4 %copy-start.1 = (f32[4,1,320,320]{3,2,1,0:T(8,128)S(1)}, f32[4,1,320,320]{3,2,1,0:T(8,128)}, u32[]{:S(2)}) copy-start(f32[4,1,320,320]{3,2,1,0:T(8,128)} %param.9) | copy-start | bytes 4915204
  6.5 84.4 %all-gather.5.cloned.1.call-start = ((), (), s32[]{:S(2)}) async-start(), calls=%async_computation | async-start | bytes 8355840 | tf_op jit(solution)/shard_map/all_gather | solution.py:9
  9.0 7.0 %copy-start.3 = (f32[4,1,320]{2,1,0:T(1,128)S(1)}, f32[4,1,320]{2,1,0:T(1,128)}, u32[]{:S(2)}) copy-start(f32[4,1,320]{2,1,0:T(1,128)} %param.8) | copy-start | bytes 15364
  12.0 5.7 %copy-start.4 = (u32[32]{0:T(128)S(1)}, u32[32]{0:T(128)}, u32[]{:S(2)}) copy-start(u32[32]{0:T(128)} %constant.63) | copy-start | bytes 388
  117.3 7.8 %copy-start.2 = (bf16[4,1,2,320,320]{4,3,2,1,0:T(8,128)(2,1)S(1)}, bf16[4,1,2,320,320]{4,3,2,1,0:T(8,128)(2,1)}, u32[]{:S(2)}) copy-start(bf16[4,1,2,320,320]{4,3,2,1,0:T(8,128)(2,1)} %param.11) | copy-start | bytes 4915204
  119.6 3.9 %collective-permute-start = (f32[1,320]{1,0:T(1,128)S(1)}, f32[1,320]{1,0:T(1,128)S(1)}, u32[]{:S(2)}, u32[]{:S(2)}) collective-permute-start(f32[1,320]{1,0:T(1,128)S(1)} %sub.83), channel_id=1, source_target_pairs={{0,30},{2,0},{4,2},{6,4},{8,6},{10,8},{12,10},{14,12},{16,14},{18,... | collective-permute-start | bytes 3848 | tf_op jit(solution)/shard_map/ppermute | solution.py:29
  121.4 3.7 %collective-permute-start.2 = (f32[4,1,320]{2,1,0:T(1,128)S(1)}, f32[4,1,320]{2,1,0:T(1,128)S(1)}, u32[]{:S(2)}, u32[]{:S(2)}) collective-permute-start(f32[4,1,320]{2,1,0:T(1,128)S(1)} %constant_dynamic-update-slice_fusion), channel_id=1, source_target_pairs={{1,0},{0,1},{3,2},{2,3},{5,4},{4,5},{7,6},{6,7},{9,8},{8,9},{11,10... | collective-permute-start | bytes 15368 | tf_op jit(solution)/shard_map/ppermute | solution.py:41
  122.9 3.6 %collective-permute-start.1 = (f32[4,1,320]{2,1,0:T(1,128)S(1)}, f32[4,1,320]{2,1,0:T(1,128)S(1)}, u32[]{:S(2)}, u32[]{:S(2)}) collective-permute-start(f32[4,1,320]{2,1,0:T(1,128)S(1)} %constant_dynamic-update-slice_fusion), channel_id=1, source_target_pairs={{0,1},{1,0},{2,3},{3,2},{4,5},{5,4},{6,7},{7,6},{8,9},{9,8},{10,11... | collective-permute-start | bytes 15368 | tf_op jit(solution)/shard_map/ppermute | solution.py:38
Sparse Core Ops, SparseCore 0:
  16.0 74.8 all-gather.4
where the time goes:
time: 263 us; the launch traced here: 261 us
  blocking collectives  124 us (47%)
  matrix products  103 us (39%)
  between operations  14.4 us (5%)
  waiting for transfers between devices  7.95 us (3%)
  local copies, waits for them, and re-layouts  4.3 us (2%)
  starting transfers between devices  3.82 us (1%)
    unnamed x2, blocking collectives  124 us
    dot_general x51, matrix products, apply_block(): jnp.einsum('...bc,...c->...b', blocks.astype(jnp.float32), vector, precis...  61.7 us
    dot_general x19, matrix products, compose(): jnp.einsum('lbc,lcd->lbd', later, earlier, precision=lax.Precision.HIGHEST)  41.2 us
    all_gather x1, waiting for transfers between devices, carried_in(): everything = jax.tree.map(lambda part: lax.all_gather(part, axis), x)  6.79 us
  transfers between devices with their start and end apart: 4, of which 3 were waited for; matrix products, arithmetic and copies ran while one was open for 2% of the time, Pallas kernels for 0%

commit v1 on v0

v1 whole, which is shorter than its diff:
```python
import functools

import jax
import jax.numpy as jnp
from jax import lax
from jax.experimental import pallas as pl
from jax.experimental.pallas import tpu as pltpu
from jax.sharding import PartitionSpec as P

F32 = jnp.float32
BF16 = jnp.bfloat16
MESH = pl.DeviceIdType.MESH
GROUP = 4
NT = (((1,), (1,)), ((), ()))
NN = (((1,), (0,)), ((), ()))


def rows_of(x):
    high = x.astype(BF16).astype(F32)
    row = lax.broadcasted_iota(jnp.int32, (16, x.shape[1]), 0)
    both = jnp.where(row == 0, high, jnp.where(row == 1, x - high, 0.0))
    return both.astype(BF16)


def product(rows, *parts):
    total = None
    for part in parts:
        term = lax.dot_general(rows, part, NT, preferred_element_type=F32)
        total = term if total is None else total + term
    return jnp.sum(total, axis=0, keepdims=True)


def split(a):
    high = a.astype(BF16)
    return high, (a - high.astype(F32)).astype(BF16)


def compose(later, earlier):
    def dot(a, b):
        return lax.dot_general(a, b, NN, preferred_element_type=F32)

    return (
        dot(later[0], earlier[1]) + dot(later[1], earlier[0]) + dot(later[0], earlier[0])
    )


def kernel(
    streams, spans, rhs_ref, lower_hbm, upper_hbm, span_hbm, out_ref,
    lower, upper, spanb, low_hi, low_lo, maps, maps_hi, maps_lo, group_hi, group_lo,
    offs, vec, start_state, first, down, side, stage,
    load_sem, send_sem, recv_sem,
):
    d = lax.axis_index("stream")
    j = lax.axis_index("span")
    slabs = lower.shape[0]
    size = lower.shape[1]
    half = size // 2
    groups = streams // GROUP
    bit0 = lax.rem(d, 2)
    bit1 = lax.rem(d // 2, 2)
    group = d // GROUP
    pair0 = (d + 1 - 2 * bit0, j)
    pair1 = (d + 2 - 4 * bit1, j)
    ahead = (lax.rem(d + GROUP, streams), j)
    behind = (lax.rem(d + streams - GROUP, streams), j)
    prev = (lax.rem(d + streams - 1, streams), j)
    following = (lax.rem(d + 1, streams), j)
    right = (d, lax.rem(j + 1, spans))
    left = (d, lax.rem(j + spans - 1, spans))

    loads = []
    for i in range(slabs):
        loads.append(pltpu.make_async_copy(lower_hbm.at[i, 0], lower.at[i], load_sem.at[i]))
    loads.append(pltpu.make_async_copy(upper_hbm.at[:, 0], upper, load_sem.at[slabs]))
    loads.append(pltpu.make_async_copy(span_hbm.at[:, 0], spanb, load_sem.at[slabs + 1]))
    for load in loads:
        load.start()

    barrier = pltpu.get_barrier_semaphore()
    partners = [pair0, pair1, ahead, behind, prev, following, right]
    if spans > 2:
        partners.append(left)
    for partner in partners:
        pl.semaphore_signal(barrier, inc=1, device_id=partner, device_id_type=MESH)

    def send(src, dst, number, to, recv_number=None):
        copy = pltpu.make_async_remote_copy(
            src_ref=src, dst_ref=dst, send_sem=send_sem.at[number],
            recv_sem=recv_sem.at[number if recv_number is None else recv_number],
            device_id=to, device_id_type=MESH,
        )
        copy.start()
        return copy

    for i in range(slabs):
        loads[i].wait()
        high, low = split(lower[i])
        low_hi[i] = high
        low_lo[i] = low

    parts = [(low_hi[i], low_lo[i]) for i in range(slabs)]
    while len(parts) > 1:
        following_parts = []
        for k in range(0, len(parts) - 1, 2):
            whole = compose(parts[k + 1], parts[k])
            if len(parts) == 2:
                break
            following_parts.append(split(whole))
        else:
            if len(parts) % 2:
                following_parts.append(parts[-1])
            parts = following_parts
            continue
        break
    if slabs == 1:
        whole = lower[0]
    if slabs % 2:
        whole = -whole
    maps[0, bit0] = whole
    pl.semaphore_wait(barrier, len(partners))
    map_copy = send(maps.at[0, bit0], maps.at[0, bit0], 0, pair0)

    def chain(begin, keep):
        state = begin
        for i in range(slabs):
            if state is None:
                state = offs[i]
            else:
                state = offs[i] - product(rows_of(state), low_hi[i], low_lo[i])
            if keep is not None:
                keep(i, state)
        return state

    def level_product(level, slot, x):
        return product(rows_of(x), maps_hi[level, slot], maps_lo[level, slot])

    def descend(sweep, state):
        wide = jnp.where(bit1 == 1, level_product(1, 0, state) + vec[sweep, 1, 0], state)
        return jnp.where(bit0 == 1, level_product(0, 0, wide) + vec[sweep, 0, 0], wide)

    offs[...] = rhs_ref[...]
    vec[0, 0, bit0] = chain(None, None)
    vec_copies = [send(vec.at[0, 0, bit0], vec.at[0, 0, bit0], 3, pair0)]
    map_copy.wait()
    for slot in range(2):
        high, low = split(maps[0, slot])
        maps_hi[0, slot] = high
        maps_lo[0, slot] = low
    maps[1, bit1] = compose((maps_hi[0, 1], maps_lo[0, 1]), (maps_hi[0, 0], maps_lo[0, 0]))
    mine = pl.ds(bit0 * half, half)
    half_copy = send(maps.at[1, bit1, mine], maps.at[1, bit1, mine], 1, pair1)
    vec_copies[0].wait()
    vec[0, 1, bit1] = vec[0, 0, 1] + level_product(0, 1, vec[0, 0, 0])
    vec_copies.append(send(vec.at[0, 1, bit1], vec.at[0, 1, bit1], 4, pair1))
    half_copy.wait()
    forward_copy = send(
        maps.at[1, 1 - bit1, mine], maps.at[1, 1 - bit1, mine], 2, pair0
    )
    vec_copies[1].wait()
    forward_copy.wait()
    for slot in range(2):
        high, low = split(maps[1, slot])
        maps_hi[1, slot] = high
        maps_lo[1, slot] = low
    shift = vec[0, 1, 1] + level_product(1, 1, vec[0, 1, 0])

    arrival = (group + 1) // groups
    chain_first = pltpu.make_async_remote_copy(
        src_ref=stage.at[0], dst_ref=start_state.at[arrival], send_sem=send_sem.at[7],
        recv_sem=recv_sem.at[7 + arrival], device_id=ahead, device_id_type=MESH,
    )

    def arrived(slot):
        return pltpu.make_async_remote_copy(
            src_ref=stage.at[slot], dst_ref=start_state.at[slot],
            send_sem=send_sem.at[7 + slot], recv_sem=recv_sem.at[7 + slot],
            device_id=ahead, device_id_type=MESH,
        )

    @pl.when(group == 0)
    def _():
        start_state[0] = jnp.zeros((1, size), F32)
        stage[0] = shift
        chain_first.start()

    whole_map = compose((maps_hi[1, 1], maps_lo[1, 1]), (maps_hi[1, 0], maps_lo[1, 0]))
    high, low = split(whole_map)
    group_hi[...] = high
    group_lo[...] = low

    @pl.when(group > 0)
    def _():
        arrived(0).wait_recv()
        stage[0] = shift + product(rows_of(start_state[0]), group_hi[...], group_lo[...])
        chain_first.start()

    def keep_first(i, state):
        first[i] = state

    chain(descend(0, start_state[0]), keep_first)
    side_copies = [send(first, side.at[0], 9, right)]
    if spans > 2:
        side_copies.append(send(first, side.at[1], 10, left))
    down_copy = send(first.at[0], down, 11, prev)
    loads[slabs].wait()
    loads[slabs + 1].wait()
    for copy in side_copies:
        copy.wait()
    down_copy.wait()
    for i in range(slabs):
        downstream = first[i + 1] if i + 1 < slabs else down[...]
        below = rows_of(side[0, i])
        above = below if spans <= 2 else rows_of(side[1, i])
        offs[i] = (
            rhs_ref[i] - product(rows_of(downstream), upper[i])
            - product(below, spanb[i, 0]) - product(above, spanb[i, 1])
        )

    vec[1, 0, bit0] = chain(None, None)
    copy = send(vec.at[1, 0, bit0], vec.at[1, 0, bit0], 5, pair0)
    copy.wait()
    vec[1, 1, bit1] = vec[1, 0, 1] + level_product(0, 1, vec[1, 0, 0])
    copy = send(vec.at[1, 1, bit1], vec.at[1, 1, bit1], 6, pair1)
    copy.wait()
    shift = vec[1, 1, 1] + level_product(1, 1, vec[1, 1, 0])
    arrived(1).wait_recv()

    @pl.when(group < groups - 1)
    def _():
        stage[1] = shift + product(rows_of(start_state[1]), group_hi[...], group_lo[...])
        arrived(1).start()

    def keep_out(i, state):
        out_ref[i] = state

    chain(descend(1, start_state[1]), keep_out)
    chain_first.wait_send()

    @pl.when(group < groups - 1)
    def _():
        arrived(1).wait_send()


def solution(mesh):
    streams, spans = mesh.shape["stream"], mesh.shape["span"]

    def shards(rhs, lower_block, upper_block, span_block):
        slabs, _, size = rhs.shape
        return pl.pallas_call(
            functools.partial(kernel, streams, spans),
            out_shape=jax.ShapeDtypeStruct((slabs, 1, size), F32),
            in_specs=[
                pl.BlockSpec(memory_space=pltpu.VMEM),
                pl.BlockSpec(memory_space=pl.ANY),
                pl.BlockSpec(memory_space=pl.ANY),
                pl.BlockSpec(memory_space=pl.ANY),
            ],
            out_specs=pl.BlockSpec(memory_space=pltpu.VMEM),
            scratch_shapes=[
                pltpu.VMEM((slabs, size, size), F32),
                pltpu.VMEM((slabs, size, size), BF16),
                pltpu.VMEM((slabs, 2, size, size), BF16),
                pltpu.VMEM((slabs, size, size), BF16),
                pltpu.VMEM((slabs, size, size), BF16),
                pltpu.VMEM((2, 2, size, size), F32),
                pltpu.VMEM((2, 2, size, size), BF16),
                pltpu.VMEM((2, 2, size, size), BF16),
                pltpu.VMEM((size, size), BF16),
                pltpu.VMEM((size, size), BF16),
                pltpu.VMEM((slabs, 1, size), F32),
                pltpu.VMEM((2, 2, 2, 1, size), F32),
                pltpu.VMEM((2, 1, size), F32),
                pltpu.VMEM((slabs, 1, size), F32),
                pltpu.VMEM((1, size), F32),
                pltpu.VMEM((2, slabs, 1, size), F32),
                pltpu.VMEM((2, 1, size), F32),
                pltpu.SemaphoreType.DMA((slabs + 2,)),
                pltpu.SemaphoreType.DMA((12,)),
                pltpu.SemaphoreType.DMA((12,)),
            ],
            compiler_params=pltpu.CompilerParams(
                collective_id=0, has_side_effects=True, vmem_limit_bytes=40 * 1024 * 1024
            ),
        )(rhs, lower_block, upper_block, span_block)

    return jax.shard_map(
        shards,
        mesh=mesh,
        in_specs=(
            P("stream", "span", None),
            P("stream", "span", None, None),
            P("stream", "span", None, None),
            P("stream", "span", None, None, None),
        ),
        out_specs=P("stream", "span", None),
        check_vma=False,
    )
```

time: 263 us -> 45.3 us (0.17)
  the two profiles are of different devices: /device:TPU:0 before, /device:TPU:24 now
where the time goes in v1:
time: 45.3 us; the launch traced here: 45.1 us
  Pallas kernels  39.5 us (87%)
  local copies, waits for them, and re-layouts  5.58 us (12%)
    pallas_call x1, Pallas kernels, shards(): pl.pallas_call(functools.partial(kernel, streams, spans), out_shape=jax.S...  39.5 us
    unnamed x9, local copies, waits for them, and re-layouts  5.58 us

profile of v1, /device:TPU:24, one launch (start us, length us, event | category | flops | bytes accessed | tf_op | source)
XLA Modules:
  0.0 45.1 jit_solution(2640840125526979269)
XLA Ops:
  0.0 0.0 copy-start
  0.0 1.5 %copy-done = f32[4,1,320,320]{3,2,1,0:T(8,128)S(1)} copy-done((f32[4,1,320,320]{3,2,1,0:T(8,128)S(1)}, f32[4,1,320,320]{3,2,1,0:T(8,128)}, u32[]{:S(2)}) %copy-start) | copy-done | bytes 1638424
  1.5 0.0 copy-start.1
  1.5 1.5 %copy-done.1 = bf16[4,1,2,320,320]{4,3,2,1,0:T(8,128)(2,1)S(1)} copy-done((bf16[4,1,2,320,320]{4,3,2,1,0:T(8,128)(2,1)S(1)}, bf16[4,1,2,320,320]{4,3,2,1,0:T(8,128)(2,1)}, u32[]{:S(2)}) %copy-start.1) | copy-done | bytes 1638424
  3.1 0.0 copy-start.2
  3.1 1.2 %copy-done.2 = bf16[4,1,320,320]{3,2,1,0:T(8,128)(2,1)S(1)} copy-done((bf16[4,1,320,320]{3,2,1,0:T(8,128)(2,1)S(1)}, bf16[4,1,320,320]{3,2,1,0:T(8,128)(2,1)}, u32[]{:S(2)}) %copy-start.2) | copy-done | bytes 819224
  4.3 0.0 copy-start.3
  4.3 0.7 %copy-done.3 = f32[4,1,320]{2,1,0:T(1,128)S(1)} copy-done((f32[4,1,320]{2,1,0:T(1,128)S(1)}, f32[4,1,320]{2,1,0:T(1,128)}, u32[]{:S(2)}) %copy-start.3) | copy-done | bytes 5144
  5.0 39.5 %shard_map.46 = f32[4,1,320]{2,1,0:T(1,128)S(1)} custom-call(f32[4,1,320]{2,1,0:T(1,128)S(1)} %copy-done.3, f32[4,1,320,320]{3,2,1,0:T(8,128)S(1)} %copy-done, bf16[4,1,320,320]{3,2,1,0:T(8,128)(2,1)S(1)} %copy-done.2, bf16[4,1,2,320,320]{4,3,2,1,0:T(8,128)(2,1)S(1)} %copy-done.1), custom_call_target="tpu_custom_call" | custom-call | tf_op jit(solution)/shard_map/pallas_call | solution.py:249
  44.5 0.6 %copy.6 = f32[4,1,320]{2,1,0:T(1,128)} copy(f32[4,1,320]{2,1,0:T(1,128)S(1)} %shard_map.46) | data formatting | bytes 10240
Async XLA Ops:
  0.0 1.5 %copy-start = (f32[4,1,320,320]{3,2,1,0:T(8,128)S(1)}, f32[4,1,320,320]{3,2,1,0:T(8,128)}, u32[]{:S(2)}) copy-start(f32[4,1,320,320]{3,2,1,0:T(8,128)} %lower_hbm.1) | copy-start | bytes 4915204
  1.5 1.5 %copy-start.1 = (bf16[4,1,2,320,320]{4,3,2,1,0:T(8,128)(2,1)S(1)}, bf16[4,1,2,320,320]{4,3,2,1,0:T(8,128)(2,1)}, u32[]{:S(2)}) copy-start(bf16[4,1,2,320,320]{4,3,2,1,0:T(8,128)(2,1)} %span_hbm.1) | copy-start | bytes 4915204
  3.1 1.2 %copy-start.2 = (bf16[4,1,320,320]{3,2,1,0:T(8,128)(2,1)S(1)}, bf16[4,1,320,320]{3,2,1,0:T(8,128)(2,1)}, u32[]{:S(2)}) copy-start(bf16[4,1,320,320]{3,2,1,0:T(8,128)(2,1)} %upper_hbm.1) | copy-start | bytes 2457604
  4.3 0.7 %copy-start.3 = (f32[4,1,320]{2,1,0:T(1,128)S(1)}, f32[4,1,320]{2,1,0:T(1,128)}, u32[]{:S(2)}) copy-start(f32[4,1,320]{2,1,0:T(1,128)} %rhs_ref.1) | copy-start | bytes 15364

commit v2 on v1

v2 whole, which is shorter than its diff:
```python
import functools

import jax
import jax.numpy as jnp
from jax import lax
from jax.experimental import pallas as pl
from jax.experimental.pallas import tpu as pltpu
from jax.sharding import PartitionSpec as P

F32 = jnp.float32
BF16 = jnp.bfloat16
MESH = pl.DeviceIdType.MESH
GROUP = 4
NT = (((1,), (1,)), ((), ()))
NN = (((1,), (0,)), ((), ()))


def columns(a, x):
    return jnp.sum(a * x, axis=1, keepdims=True)


def as_row(column):
    size = column.shape[0]
    pieces = []
    for begin in range(0, size, 128):
        count = min(128, size - begin)
        row = lax.broadcasted_iota(jnp.int32, (count, count), 0)
        lane = lax.broadcasted_iota(jnp.int32, (count, count), 1)
        part = jnp.where(row == lane, column[begin : begin + count], 0.0)
        pieces.append(jnp.sum(part, axis=0, keepdims=True))
    return jnp.concatenate(pieces, axis=1)


def product(a, x):
    return as_row(columns(a, x))


def split(a):
    high = a.astype(BF16)
    return high, (a - high.astype(F32)).astype(BF16)


def compose(later, earlier):
    def dot(a, b):
        return lax.dot_general(a, b, NN, preferred_element_type=F32)

    return (
        dot(later[0], earlier[1]) + dot(later[1], earlier[0]) + dot(later[0], earlier[0])
    )


def kernel(
    streams, spans, rhs_hbm, lower_hbm, upper_hbm, span_hbm, out_ref,
    rhs, lower, upper, spanb, upper_wide, span_wide, maps, group_map,
    offs, vec, start_state, middle, first, down, side, stage,
    load_sem, send_sem, recv_sem,
):
    d = lax.axis_index("stream")
    j = lax.axis_index("span")
    slabs = lower.shape[0]
    size = lower.shape[1]
    half = size // 2
    groups = streams // GROUP
    early = min(2, groups - 1)
    bit0 = lax.rem(d, 2)
    bit1 = lax.rem(d // 2, 2)
    group = d // GROUP
    other = 2 - 4 * bit1
    pair0 = (d + 1 - 2 * bit0, j)
    pair1 = (d + other, j)
    ahead = (lax.rem(d + GROUP, streams), j)
    behind = (lax.rem(d + streams - GROUP, streams), j)
    ahead_pair = (lax.rem(d + GROUP, streams) + other, j)
    behind_pair = (lax.rem(d + streams - GROUP, streams) + other, j)
    prev = (lax.rem(d + streams - 1, streams), j)
    following = (lax.rem(d + 1, streams), j)
    right = (d, lax.rem(j + 1, spans))
    left = (d, lax.rem(j + spans - 1, spans))

    loads = []
    for i in range(slabs):
        loads.append(pltpu.make_async_copy(lower_hbm.at[i, 0], lower.at[i], load_sem.at[i]))
    rhs_load = pltpu.make_async_copy(rhs_hbm, rhs, load_sem.at[slabs + 2])
    upper_load = pltpu.make_async_copy(upper_hbm.at[:, 0], upper, load_sem.at[slabs])
    span_load = pltpu.make_async_copy(span_hbm.at[:, 0], spanb, load_sem.at[slabs + 1])
    loads[0].start()
    rhs_load.start()
    for load in loads[1:]:
        load.start()
    upper_load.start()
    span_load.start()

    barrier = pltpu.get_barrier_semaphore()
    partners = [
        pair0, pair1, ahead, behind, ahead_pair, behind_pair, prev, following, right
    ]
    if spans > 2:
        partners.append(left)
    for partner in partners:
        pl.semaphore_signal(barrier, inc=1, device_id=partner, device_id_type=MESH)

    def remote(src, dst, number, to, recv_number=None):
        return pltpu.make_async_remote_copy(
            src_ref=src, dst_ref=dst, send_sem=send_sem.at[number],
            recv_sem=recv_sem.at[number if recv_number is None else recv_number],
            device_id=to, device_id_type=MESH,
        )

    def send(src, dst, number, to):
        copy = remote(src, dst, number, to)
        copy.start()
        return copy

    parts = []
    for i in range(slabs):
        loads[i].wait()
        part = split(lower[i])
        if i % 2:
            whole = compose(part, pending)
            if slabs > 2:
                parts.append(split(whole))
        else:
            pending = part
    if slabs == 1:
        whole = lower[0]
    elif slabs > 2:
        if slabs % 2:
            parts.append(pending)
        rest = parts[0]
        for k in range(1, len(parts)):
            whole = compose(parts[k], rest)
            if k < len(parts) - 1:
                rest = split(whole)
    if slabs % 2:
        whole = -whole
    maps[0, bit0] = whole
    pl.semaphore_wait(barrier, len(partners))
    map_copy = send(maps.at[0, bit0], maps.at[0, bit0], 0, pair0)

    def chain(begin, keep):
        state = begin
        for i in range(slabs):
            if state is None:
                state = offs[i]
            else:
                state = offs[i] - product(lower[i], state)
            if keep is not None:
                keep(i, state)
        return state

    def descend(sweep, state):
        wide = jnp.where(bit1 == 1, product(maps[1, 0], state) + vec[sweep, 1, 0], state)
        return jnp.where(bit0 == 1, product(maps[0, 0], wide) + vec[sweep, 0, 0], wide)

    rhs_load.wait()
    offs[...] = rhs[...]
    vec[0, 0, bit0] = chain(None, None)
    pair0_copy = send(vec.at[0, 0, bit0], vec.at[0, 0, bit0], 3, pair0)
    map_copy.wait_recv()
    pair_map = compose(split(maps[0, 1]), split(maps[0, 0]))
    maps[1, bit1] = pair_map
    mine = pl.ds(bit0 * half, half)
    half_copy = send(maps.at[1, bit1, mine], maps.at[1, bit1, mine], 1, pair1)
    pair0_copy.wait_recv()
    vec[0, 1, bit1] = vec[0, 0, 1] + product(maps[0, 1], vec[0, 0, 0])
    pair1_copy = send(vec.at[0, 1, bit1], vec.at[0, 1, bit1], 4, pair1)

    upper_load.wait()
    span_load.wait()
    for i in range(slabs):
        upper_wide[i] = upper[i].astype(F32)
        if spans <= 2:
            span_wide[i] = spanb[i, 0].astype(F32) + spanb[i, 1].astype(F32)

    arrival = (group + 1) // groups
    chain_first = remote(stage.at[0], start_state.at[arrival], 7, ahead, 7 + arrival)
    chain_other = remote(stage.at[0], start_state.at[0], 12, ahead_pair, 7)
    middle_copy = remote(stage.at[2], middle, 13, pair1)

    def arrived(slot):
        return remote(stage.at[slot], start_state.at[slot], 7 + slot, ahead)

    pair1_copy.wait_recv()

    @pl.when(group == 0)
    def _():
        start_state[0] = jnp.zeros((1, size), F32)

    @pl.when((group == 0) & (bit1 == 1))
    def _():
        stage[0] = vec[0, 1, 1] + product(maps[1, 1], vec[0, 1, 0])
        chain_first.start()
        chain_other.start()

    if early > 1:
        @pl.when((group == 1) & (bit1 == 0))
        def _():
            arrived(0).wait_recv()
            stage[2] = vec[0, 1, 0] + product(maps[1, 0], start_state[0])
            middle_copy.start()

        @pl.when((group == 1) & (bit1 == 1))
        def _():
            middle_copy.wait_recv()
            stage[0] = vec[0, 1, 1] + product(maps[1, 1], middle[...])
            chain_first.start()
            chain_other.start()
            arrived(0).wait_recv()

    half_copy.wait_recv()
    forward_copy = send(
        maps.at[1, 1 - bit1, mine], maps.at[1, 1 - bit1, mine], 2, pair0
    )
    forward_copy.wait_recv()
    shift = vec[0, 1, 1] + product(maps[1, 1], vec[0, 1, 0])
    group_map[...] = compose(split(maps[1, 1]), split(maps[1, 0]))

    @pl.when(group >= early)
    def _():
        arrived(0).wait_recv()
        stage[0] = shift + product(group_map[...], start_state[0])
        chain_first.start()

    def keep_first(i, state):
        first[i] = state

    chain(descend(0, start_state[0]), keep_first)
    side_copies = [send(first, side.at[0], 9, right)]
    if spans > 2:
        side_copies.append(send(first, side.at[1], 10, left))
    down_copy = send(first.at[0], down, 11, prev)
    for copy in side_copies:
        copy.wait_recv()
    down_copy.wait_recv()
    for i in range(slabs):
        total = upper_wide[i] * (first[i + 1] if i + 1 < slabs else down[...])
        if spans <= 2:
            total = total + span_wide[i] * side[0, i]
        else:
            total = total + spanb[i, 0].astype(F32) * side[0, i]
            total = total + spanb[i, 1].astype(F32) * side[1, i]
        offs[i] = rhs[i] - as_row(jnp.sum(total, axis=1, keepdims=True))

    vec[1, 0, bit0] = chain(None, None)
    second0 = send(vec.at[1, 0, bit0], vec.at[1, 0, bit0], 5, pair0)
    second0.wait_recv()
    vec[1, 1, bit1] = vec[1, 0, 1] + product(maps[0, 1], vec[1, 0, 0])
    second1 = send(vec.at[1, 1, bit1], vec.at[1, 1, bit1], 6, pair1)
    second1.wait_recv()
    shift = vec[1, 1, 1] + product(maps[1, 1], vec[1, 1, 0])
    arrived(1).wait_recv()

    @pl.when(group < groups - 1)
    def _():
        stage[1] = shift + product(group_map[...], start_state[1])
        arrived(1).start()

    def keep_out(i, state):
        out_ref[i] = state

    chain(descend(1, start_state[1]), keep_out)
    for copy in side_copies + [
        map_copy, half_copy, forward_copy, pair0_copy, pair1_copy, down_copy, second0, second1
    ]:
        copy.wait_send()

    @pl.when((group >= early) | (bit1 == 1))
    def _():
        chain_first.wait_send()

    @pl.when((group < early) & (bit1 == 1))
    def _():
        chain_other.wait_send()

    if early > 1:
        @pl.when((group == 1) & (bit1 == 0))
        def _():
            middle_copy.wait_send()

    @pl.when(group < groups - 1)
    def _():
        arrived(1).wait_send()


def solution(mesh):
    streams, spans = mesh.shape["stream"], mesh.shape["span"]

    def shards(rhs, lower_block, upper_block, span_block):
        slabs, _, size = rhs.shape
        return pl.pallas_call(
            functools.partial(kernel, streams, spans),
            out_shape=jax.ShapeDtypeStruct((slabs, 1, size), F32),
            in_specs=[pl.BlockSpec(memory_space=pltpu.HBM)] * 4,
            out_specs=pl.BlockSpec(memory_space=pltpu.VMEM),
            scratch_shapes=[
                pltpu.VMEM((slabs, 1, size), F32),
                pltpu.VMEM((slabs, size, size), F32),
                pltpu.VMEM((slabs, size, size), BF16),
                pltpu.VMEM((slabs, 2, size, size), BF16),
                pltpu.VMEM((slabs, size, size), F32),
                pltpu.VMEM((slabs, size, size), F32),
                pltpu.VMEM((2, 2, size, size), F32),
                pltpu.VMEM((size, size), F32),
                pltpu.VMEM((slabs, 1, size), F32),
                pltpu.VMEM((2, 2, 2, 1, size), F32),
                pltpu.VMEM((2, 1, size), F32),
                pltpu.VMEM((1, size), F32),
                pltpu.VMEM((slabs, 1, size), F32),
                pltpu.VMEM((1, size), F32),
                pltpu.VMEM((2, slabs, 1, size), F32),
                pltpu.VMEM((3, 1, size), F32),
                pltpu.SemaphoreType.DMA((slabs + 3,)),
                pltpu.SemaphoreType.DMA((14,)),
                pltpu.SemaphoreType.DMA((14,)),
            ],
            compiler_params=pltpu.CompilerParams(
                collective_id=0, has_side_effects=True, vmem_limit_bytes=63 * 1024 * 1024
            ),
        )(rhs, lower_block, upper_block, span_block)

    return jax.shard_map(
        shards,
        mesh=mesh,
        in_specs=(
            P("stream", "span", None),
            P("stream", "span", None, None),
            P("stream", "span", None, None),
            P("stream", "span", None, None, None),
        ),
        out_specs=P("stream", "span", None),
        check_vma=False,
    )
```

time: 45.3 us -> 38.7 us (0.85)
  local copies, waits for them, and re-layouts: 5.58 us -> 1.29 us
  Pallas kernels: 39.5 us -> 37.2 us
    unnamed x9 -> x1, local copies, waits for them, and re-layouts: 5.58 us -> 1.29 us
    pallas_call x1, Pallas kernels: 39.5 us -> 37.2 us  [shards(): pl.pallas_call(functools.partial(kernel, streams, spans), out_shape=jax.S...]
where the time goes in v2:
time: 38.7 us; the launch traced here: 38.5 us
  Pallas kernels  37.2 us (96%)
  local copies, waits for them, and re-layouts  1.29 us (3%)
    pallas_call x1, Pallas kernels, shards(): pl.pallas_call(functools.partial(kernel, streams, spans), out_shape=jax.S...  37.2 us
    unnamed x1, local copies, waits for them, and re-layouts  1.29 us

profile of v2, /device:TPU:24, one launch (start us, length us, event | category | flops | bytes accessed | tf_op | source)
XLA Modules:
  0.0 38.5 jit_solution(12786521740009239547)
XLA Ops:
  0.0 37.2 %shard_map.46 = f32[4,1,320]{2,1,0:T(1,128)} custom-call(f32[4,1,320]{2,1,0:T(1,128)} %rhs_hbm.1, f32[4,1,320,320]{3,2,1,0:T(8,128)} %lower_hbm.1, bf16[4,1,320,320]{3,2,1,0:T(8,128)(2,1)} %upper_hbm.1, bf16[4,1,2,320,320]{4,3,2,1,0:T(8,128)(2,1)} %span_hbm.1), custom_call_target="tpu_custom_call" | custom-call | tf_op jit(solution)/shard_map/pallas_call | solution.py:290
  37.2 1.3 %copy.6 = f32[4,1,320]{2,1,0:T(1,128)} copy(f32[4,1,320]{2,1,0:T(1,128)} %shard_map.46) | data formatting | bytes 10240

commit v3 on v2

--- a/solution.py
+++ b/solution.py
@@ -72,6 +72,7 @@
     behind = (lax.rem(d + streams - GROUP, streams), j)
     ahead_pair = (lax.rem(d + GROUP, streams) + other, j)
     behind_pair = (lax.rem(d + streams - GROUP, streams) + other, j)
+    across = (d + other + 1 - 2 * bit0, j)
     prev = (lax.rem(d + streams - 1, streams), j)
     following = (lax.rem(d + 1, streams), j)
     right = (d, lax.rem(j + 1, spans))
@@ -92,7 +93,8 @@
 
     barrier = pltpu.get_barrier_semaphore()
     partners = [
-        pair0, pair1, ahead, behind, ahead_pair, behind_pair, prev, following, right
+        pair0, pair1, ahead, behind, ahead_pair, behind_pair, prev, following, right,
+        across,
     ]
     if spans > 2:
         partners.append(left)
@@ -110,6 +112,21 @@
         copy = remote(src, dst, number, to)
         copy.start()
         return copy
+
+    def chain(begin, keep):
+        state = begin
+        for i in range(slabs):
+            if state is None:
+                state = offs[i]
+            else:
+                state = offs[i] - product(lower[i], state)
+            if keep is not None:
+                keep(i, state)
+        return state
+
+    def descend(sweep, state):
+        wide = jnp.where(bit1 == 1, product(maps[1, 0], state) + vec[sweep, 1, 0], state)
+        return jnp.where(bit0 == 1, product(maps[0, 0], wide) + vec[sweep, 0, 0], wide)
 
     parts = []
     for i in range(slabs):
@@ -121,6 +138,11 @@
                 parts.append(split(whole))
         else:
             pending = part
+    rhs_load.wait()
+    offs[...] = rhs[...]
+    vec[0, 0, bit0] = chain(None, None)
+    pl.semaphore_wait(barrier, len(partners))
+    pair0_copy = send(vec.at[0, 0, bit0], vec.at[0, 0, bit0], 3, pair0)
     if slabs == 1:
         whole = lower[0]
     elif slabs > 2:
@@ -134,36 +156,28 @@
     if slabs % 2:
         whole = -whole
     maps[0, bit0] = whole
-    pl.semaphore_wait(barrier, len(partners))
     map_copy = send(maps.at[0, bit0], maps.at[0, bit0], 0, pair0)
 
-    def chain(begin, keep):
-        state = begin
-        for i in range(slabs):
-            if state is None:
-                state = offs[i]
-            else:
-                state = offs[i] - product(lower[i], state)
-            if keep is not None:
-                keep(i, state)
-        return state
-
-    def descend(sweep, state):
-        wide = jnp.where(bit1 == 1, product(maps[1, 0], state) + vec[sweep, 1, 0], state)
-        return jnp.where(bit0 == 1, product(maps[0, 0], wide) + vec[sweep, 0, 0], wide)
-
-    rhs_load.wait()
-    offs[...] = rhs[...]
-    vec[0, 0, bit0] = chain(None, None)
-    pair0_copy = send(vec.at[0, 0, bit0], vec.at[0, 0, bit0], 3, pair0)
+    pair1_copy = remote(vec.at[0, 1, bit1], vec.at[0, 1, bit1], 4, pair1)
+    across_copy = remote(vec.at[0, 1, bit1], vec.at[0, 1, bit1], 14, across, 4)
+    pair0_copy.wait_recv()
+
+    @pl.when(bit0 == 1)
+    def _():
+        vec[0, 1, bit1] = vec[0, 0, 1] + product(maps[0, 1], vec[0, 0, 0])
+        pair1_copy.start()
+        across_copy.start()
+
     map_copy.wait_recv()
+
+    @pl.when(bit0 == 0)
+    def _():
+        vec[0, 1, bit1] = vec[0, 0, 1] + product(maps[0, 1], vec[0, 0, 0])
+
     pair_map = compose(split(maps[0, 1]), split(maps[0, 0]))
     maps[1, bit1] = pair_map
     mine = pl.ds(bit0 * half, half)
     half_copy = send(maps.at[1, bit1, mine], maps.at[1, bit1, mine], 1, pair1)
-    pair0_copy.wait_recv()
-    vec[0, 1, bit1] = vec[0, 0, 1] + product(maps[0, 1], vec[0, 0, 0])
-    pair1_copy = send(vec.at[0, 1, bit1], vec.at[0, 1, bit1], 4, pair1)
 
     upper_load.wait()
     span_load.wait()
@@ -260,9 +274,14 @@
 
     chain(descend(1, start_state[1]), keep_out)
     for copy in side_copies + [
-        map_copy, half_copy, forward_copy, pair0_copy, pair1_copy, down_copy, second0, second1
+        map_copy, half_copy, forward_copy, pair0_copy, down_copy, second0, second1
     ]:
         copy.wait_send()
+
+    @pl.when(bit0 == 1)
+    def _():
+        pair1_copy.wait_send()
+        across_copy.wait_send()
 
     @pl.when((group >= early) | (bit1 == 1))
     def _():
@@ -310,8 +329,8 @@
                 pltpu.VMEM((2, slabs, 1, size), F32),
                 pltpu.VMEM((3, 1, size), F32),
                 pltpu.SemaphoreType.DMA((slabs + 3,)),
-                pltpu.SemaphoreType.DMA((14,)),
-                pltpu.SemaphoreType.DMA((14,)),
+                pltpu.SemaphoreType.DMA((15,)),
+                pltpu.SemaphoreType.DMA((15,)),
             ],
             compiler_params=pltpu.CompilerParams(
                 collective_id=0, has_side_effects=True, vmem_limit_bytes=63 * 1024 * 1024

time: 38.7 us -> 33.7 us (0.87)
  Pallas kernels: 37.2 us -> 32.2 us
    pallas_call x1, Pallas kernels: 37.2 us -> 32.2 us  [shards(): pl.pallas_call(functools.partial(kernel, streams, spans), out_shape=jax.S...]
where the time goes in v3:
time: 33.7 us; the launch traced here: 33.5 us
  Pallas kernels  32.2 us (96%)
  local copies, waits for them, and re-layouts  1.29 us (4%)
    pallas_call x1, Pallas kernels, shards(): pl.pallas_call(functools.partial(kernel, streams, spans), out_shape=jax.S...  32.2 us
    unnamed x1, local copies, waits for them, and re-layouts  1.29 us

profile of v3, /device:TPU:24, one launch (start us, length us, event | category | flops | bytes accessed | tf_op | source)
XLA Modules:
  0.0 33.5 jit_solution(16026181709950125330)
XLA Ops:
  0.0 32.2 %shard_map.46 = f32[4,1,320]{2,1,0:T(1,128)} custom-call(f32[4,1,320]{2,1,0:T(1,128)} %rhs_hbm.1, f32[4,1,320,320]{3,2,1,0:T(8,128)} %lower_hbm.1, bf16[4,1,320,320]{3,2,1,0:T(8,128)(2,1)} %upper_hbm.1, bf16[4,1,2,320,320]{4,3,2,1,0:T(8,128)(2,1)} %span_hbm.1), custom_call_target="tpu_custom_call" | custom-call | tf_op jit(solution)/shard_map/pallas_call | solution.py:309
  32.2 1.3 %copy.6 = f32[4,1,320]{2,1,0:T(1,128)} copy(f32[4,1,320]{2,1,0:T(1,128)} %shard_map.46) | data formatting | bytes 10240

commit v4 on v3

--- a/solution.py
+++ b/solution.py
@@ -88,8 +88,6 @@
     rhs_load.start()
     for load in loads[1:]:
         load.start()
-    upper_load.start()
-    span_load.start()
 
     barrier = pltpu.get_barrier_semaphore()
     partners = [
@@ -138,25 +136,34 @@
                 parts.append(split(whole))
         else:
             pending = part
+    upper_load.start()
+    span_load.start()
     rhs_load.wait()
     offs[...] = rhs[...]
     vec[0, 0, bit0] = chain(None, None)
     pl.semaphore_wait(barrier, len(partners))
     pair0_copy = send(vec.at[0, 0, bit0], vec.at[0, 0, bit0], 3, pair0)
+    last = None
     if slabs == 1:
         whole = lower[0]
     elif slabs > 2:
         if slabs % 2:
             parts.append(pending)
         rest = parts[0]
-        for k in range(1, len(parts)):
-            whole = compose(parts[k], rest)
-            if k < len(parts) - 1:
-                rest = split(whole)
-    if slabs % 2:
-        whole = -whole
-    maps[0, bit0] = whole
-    map_copy = send(maps.at[0, bit0], maps.at[0, bit0], 0, pair0)
+        for k in range(1, len(parts) - 1):
+            rest = split(compose(parts[k], rest))
+        last = parts[-1]
+    map_copies = []
+    for k in range(2):
+        rows = slice(k * half, (k + 1) * half)
+        if last is None:
+            piece = whole[rows]
+        else:
+            piece = compose((last[0][rows], last[1][rows]), rest)
+        maps[0, bit0, rows] = -piece if slabs % 2 else piece
+        map_copies.append(
+            send(maps.at[0, bit0, rows], maps.at[0, bit0, rows], 15 * k, pair0)
+        )
 
     pair1_copy = remote(vec.at[0, 1, bit1], vec.at[0, 1, bit1], 4, pair1)
     across_copy = remote(vec.at[0, 1, bit1], vec.at[0, 1, bit1], 14, across, 4)
@@ -168,7 +175,8 @@
         pair1_copy.start()
         across_copy.start()
 
-    map_copy.wait_recv()
+    for copy in map_copies:
+        copy.wait_recv()
 
     @pl.when(bit0 == 0)
     def _():
@@ -273,8 +281,8 @@
         out_ref[i] = state
 
     chain(descend(1, start_state[1]), keep_out)
-    for copy in side_copies + [
-        map_copy, half_copy, forward_copy, pair0_copy, down_copy, second0, second1
+    for copy in side_copies + map_copies + [
+        half_copy, forward_copy, pair0_copy, down_copy, second0, second1
     ]:
         copy.wait_send()
 
@@ -329,8 +337,8 @@
                 pltpu.VMEM((2, slabs, 1, size), F32),
                 pltpu.VMEM((3, 1, size), F32),
                 pltpu.SemaphoreType.DMA((slabs + 3,)),
-                pltpu.SemaphoreType.DMA((15,)),
-                pltpu.SemaphoreType.DMA((15,)),
+                pltpu.SemaphoreType.DMA((16,)),
+                pltpu.SemaphoreType.DMA((16,)),
             ],
             compiler_params=pltpu.CompilerParams(
                 collective_id=0, has_side_effects=True, vmem_limit_bytes=63 * 1024 * 1024

time: 33.7 us -> 33.4 us (level)
  no operation moved by 1% of the time
where the time goes in v4:
time: 33.4 us; the launch traced here: 33.2 us
  Pallas kernels  31.9 us (96%)
  local copies, waits for them, and re-layouts  1.29 us (4%)
    pallas_call x1, Pallas kernels, shards(): pl.pallas_call(functools.partial(kernel, streams, spans), out_shape=jax.S...  31.9 us
    unnamed x1, local copies, waits for them, and re-layouts  1.29 us

profile of v4, /device:TPU:24, one launch (start us, length us, event | category | flops | bytes accessed | tf_op | source)
XLA Modules:
  0.0 33.2 jit_solution(9409940742939457135)
XLA Ops:
  0.0 31.9 %shard_map.46 = f32[4,1,320]{2,1,0:T(1,128)} custom-call(f32[4,1,320]{2,1,0:T(1,128)} %rhs_hbm.1, f32[4,1,320,320]{3,2,1,0:T(8,128)} %lower_hbm.1, bf16[4,1,320,320]{3,2,1,0:T(8,128)(2,1)} %upper_hbm.1, bf16[4,1,2,320,320]{4,3,2,1,0:T(8,128)(2,1)} %span_hbm.1), custom_call_target="tpu_custom_call" | custom-call | tf_op jit(solution)/shard_map/pallas_call | solution.py:317
  31.9 1.3 %copy.6 = f32[4,1,320]{2,1,0:T(1,128)} copy(f32[4,1,320]{2,1,0:T(1,128)} %shard_map.46) | data formatting | bytes 10240

commit v5 on v4

--- a/solution.py
+++ b/solution.py
@@ -182,10 +182,12 @@
     def _():
         vec[0, 1, bit1] = vec[0, 0, 1] + product(maps[0, 1], vec[0, 0, 0])
 
-    pair_map = compose(split(maps[0, 1]), split(maps[0, 0]))
-    maps[1, bit1] = pair_map
-    mine = pl.ds(bit0 * half, half)
+    earlier = split(maps[0, 0])
+    mine = pl.ds(pl.multiple_of(bit0 * half, 8), half)
+    rest_rows = pl.ds(pl.multiple_of((1 - bit0) * half, 8), half)
+    maps[1, bit1, mine] = compose(split(maps[0, 1, mine]), earlier)
     half_copy = send(maps.at[1, bit1, mine], maps.at[1, bit1, mine], 1, pair1)
+    maps[1, bit1, rest_rows] = compose(split(maps[0, 1, rest_rows]), earlier)
 
     upper_load.wait()
     span_load.wait()

time: 33.4 us -> 33.3 us (level)
  no operation moved by 1% of the time
where the time goes in v5:
time: 33.3 us; the launch traced here: 33.1 us
  Pallas kernels  31.8 us (95%)
  local copies, waits for them, and re-layouts  1.29 us (4%)
    pallas_call x1, Pallas kernels, shards(): pl.pallas_call(functools.partial(kernel, streams, spans), out_shape=jax.S...  31.8 us
    unnamed x1, local copies, waits for them, and re-layouts  1.29 us

profile of v5, /device:TPU:24, one launch (start us, length us, event | category | flops | bytes accessed | tf_op | source)
XLA Modules:
  0.0 33.1 jit_solution(5345606427573555334)
XLA Ops:
  0.0 31.8 %shard_map.46 = f32[4,1,320]{2,1,0:T(1,128)} custom-call(f32[4,1,320]{2,1,0:T(1,128)} %rhs_hbm.1, f32[4,1,320,320]{3,2,1,0:T(8,128)} %lower_hbm.1, bf16[4,1,320,320]{3,2,1,0:T(8,128)(2,1)} %upper_hbm.1, bf16[4,1,2,320,320]{4,3,2,1,0:T(8,128)(2,1)} %span_hbm.1), custom_call_target="tpu_custom_call" | custom-call | tf_op jit(solution)/shard_map/pallas_call | solution.py:319
  31.8 1.3 %copy.6 = f32[4,1,320]{2,1,0:T(1,128)} copy(f32[4,1,320]{2,1,0:T(1,128)} %shard_map.46) | data formatting | bytes 10240
